TPU v7x, 256 devices: a whole 4x4x8 slice. The times are simulated.
256 devices in a mesh: row: 8 (over z), col: 32 (over x, y, core).
Axes of the slice: x: 4, y: 4, z: 8, core: 2. Of those that a mesh axis runs over, the one named last changes fastest.
Arguments:
- latitude: bfloat16 [16384, 256], P(('row', 'col')), may hold values from -4 to 4
- longitude: bfloat16 [16384, 512], P(('row', 'col')), may hold values from -4 to 4
- weight: bfloat16 [16384], P(('row', 'col')), may hold values from 0.29882812 to 3
- harmonic_index: int32 [2, 24576], P(None, 'col'), may hold values from 0 to 511, as said below
Outputs:
- coefficients: float32 [512, 24576], P(None, 'col')
- residual: float32 [16384, 24576], P('row', 'col')
Inputs may be any that keep to these rules, and one draw needn't show every extreme that they name: The pairs (harmonic_index[0, j], harmonic_index[1, j]) are distinct over all 24576 columns; row 0 is below 256, and harmonic_index[1, j] // 2 never exceeds harmonic_index[0, j].
All inputs are finite; a program needn't handle non-finite values.
Results may differ from a plain program's by a relative error of at most 0.0003.
Values may be sent and summed in bfloat16 or wider, within the bound.
No kernel may reach another device: no remote copies, remote signals or barrier semaphores. Data moves between devices by JAX's collectives and lax.ppermute only.
A program may use at most 128 MiB of HBM per device.

v0:
```python
import math
import jax
import jax.numpy as jnp
from jax import lax
from jax.sharding import PartitionSpec as P

PANEL = 256


def in_one_piece(arrays, axis, dim, along):
    widths = [math.prod(a.shape[along:]) for a in arrays]
    both = jnp.concatenate(
        [a.reshape(*a.shape[:along], w) for a, w in zip(arrays, widths)], axis=along
    )
    result = lax.all_gather(both, axis, axis=dim, tiled=True)
    tiles = jnp.split(result, [sum(widths[:k]) for k in range(1, len(widths))], axis=along)
    return tuple(
        (b.reshape(*result.shape[:along], *a.shape[along:]) for a, b in zip(arrays, tiles))
    )


def picked(array, axis, root):
    return lax.dynamic_index_in_dim(lax.all_gather(array, axis), root, 0, keepdims=False)


def synthesize(latitude, longitude, weight, column_index):
    degree_hot = (
        column_index[0][None, :] == jnp.arange(latitude.shape[1], dtype=jnp.int32)[:, None]
    ).astype(jnp.bfloat16)
    order_hot = (
        column_index[1][None, :] == jnp.arange(longitude.shape[1], dtype=jnp.int32)[:, None]
    ).astype(jnp.bfloat16)
    picked_degree = jnp.dot(latitude, degree_hot, preferred_element_type=jnp.float32)
    picked_order = jnp.dot(longitude, order_hot, preferred_element_type=jnp.float32)
    return weight.astype(jnp.float32)[:, None] * picked_degree * picked_order


def orthonormal(panel_cols, gram_sum):
    lower_factor = jnp.linalg.cholesky(gram_sum)
    return lax.linalg.triangular_solve(lower_factor, panel_cols.T, left_side=True, lower=True)


def remove_span(design, basis_t, top_rows):
    return design - jnp.dot(
        basis_t.T, top_rows, precision=lax.Precision.HIGHEST, preferred_element_type=jnp.float32
    )


def shards(latitude, longitude, weight, harmonic_index):
    tables = in_one_piece((latitude, longitude, weight), "col", 0, 1)
    lead_index = picked(harmonic_index[:, : 2 * PANEL], "col", 0)
    lead_cols = synthesize(tables[0], tables[1], tables[2], lead_index)
    design = synthesize(tables[0], tables[1], tables[2], harmonic_index)
    local_gram = jnp.dot(
        lead_cols.T, lead_cols, precision=lax.Precision.HIGHEST, preferred_element_type=jnp.float32
    )
    gram_sum = lax.psum(local_gram, "row")
    basis_t = orthonormal(lead_cols, gram_sum)
    local_rows = jnp.dot(
        basis_t, design, precision=lax.Precision.HIGHEST, preferred_element_type=jnp.float32
    )
    coefficients = lax.psum(local_rows, "row")
    residual = remove_span(design, basis_t, coefficients)
    return (coefficients, residual)


def solution(mesh):
    return jax.shard_map(
        shards,
        mesh=mesh,
        in_specs=(
            P(("row", "col"), None),
            P(("row", "col"), None),
            P(("row", "col")),
            P(None, "col"),
        ),
        out_specs=(P(None, "col"), P("row", "col")),
        check_vma=False,
    )
```

profile of v0, /device:TPU:2, one launch (start us, length us, event | category | flops | bytes accessed | tf_op | source)
XLA Modules:
  0.0 433.0 jit_solution(3629395771598168058)
XLA Ops:
  7.2 0.0 all-gather.4.cloned.1.call-start
  7.2 0.8 copy.12
  8.0 1.5 pad_maximum_fusion.3
  9.5 0.0 all-gather.4.cloned.1.call-update
  9.5 0.0 all-reduce.4.cloned.1.call-start
  9.5 0.7 slice_bitcast_fusion.8
  10.2 24.6 %all-gather.1 = s32[32,2,512]{2,1,0:T(2,128)S(1)} all-gather(s32[1,2,512]{2,1,0:T(2,128)S(1)} %slice_bitcast_fusion.8), channel_id=2, replica_groups=mesh['row'=8,'col'=32] {'col'}, dimensions={0}, use_global_device_ids=true | all-gather | bytes 135168 | tf_op jit(solution)/shard_map/all_gather | solution.py:23
  34.8 0.8 slice_reduce_fusion
  35.6 28.7 %all-gather.4.cloned.1.call-done = bf16[2048,769]{1,0:T(8,128)(2,1)} async-done(((bf16[64,769]{1,0:T(8,128)(2,1)}), bf16[2048,769]{1,0:T(8,128)(2,1)}) %all-gather.4.cloned.1.call-update) | async-done | bytes 3149840 | tf_op jit(solution)/shard_map/all_gather | solution.py:15
  64.3 1.4 convert_reduce_fusion
  65.7 2.0 fusion.20
  67.7 1.3 multiply_multiply_fusion.1
  69.0 1.9 copy-done
  70.9 8.0 %fusion.49 = f32[512,512]{0,1:T(8,128)} fusion(f32[2048,512]{1,0:T(8,128)S(1)} %multiply_multiply_fusion.1), kind=kOutput, calls=%fused_computation.94 | convolution fusion | flops 6442450944 | bytes 5242880 | tf_op jit(solution)/shard_map/dot_general | solution.py:54
  79.0 0.3 all-reduce.6.cloned.1.call-start
  79.3 2.4 fusion.18
  81.7 4.7 %multiply_multiply_fusion = f32[2048,768]{1,0:T(8,128)} fusion(f32[2048,768]{1,0:T(8,128)S(1)} %fusion.18, f32[2048]{0:T(1024)S(1)} %convert_reduce_fusion, bf16[2048,769]{1,0:T(8,128)(2,1)S(1)} %copy-done.3, s32[768]{0:T(1024)S(1)} %get-tuple-element.10), kind=kOutput, calls=%fused_computation.2 | convolution fusion | flops 1614151680 | bytes 14692352 | tf_op jit(solution)/shard_map/dot_general | solution.py:34
  86.4 68.5 %all-reduce.4.cloned.1.call-done = f32[512,512]{0,1:T(8,128)} async-done(((f32[512,512]{0,1:T(8,128)}), f32[512,512]{0,1:T(8,128)}) %all-reduce.4.cloned.1.call-update) | async-done | bytes 1048592 | tf_op jit(solution)/shard_map/psum | solution.py:57
  154.9 1.6 copy.14
  156.4 1.4 fusion.17
  157.9 11.7 %cholesky.104 = f32[128,128]{1,0:T(8,128)S(1)} custom-call(f32[128,128]{1,0:T(8,128)S(1)} %cholesky.266), custom_call_target="Cholesky" | custom-call | tf_op jit(solution)/shard_map/jit(cholesky)/cholesky | solution.py:39
  169.6 9.8 %custom-call.30 = f32[1,128,128]{1,2,0:T(8,128)S(1)} custom-call(f32[1,128,128]{2,1,0:T(8,128)S(1)} %get-tuple-element.33), custom_call_target="InvertDiagBlocksLowerTriangular" | custom-call | tf_op jit(solution)/shard_map/jit(cholesky)/cholesky | solution.py:39
  179.5 0.1 cholesky.224
  179.6 0.3 constant_dynamic-update-slice_fusion.3
  179.9 0.3 convolution_subtract_fusion.3
  180.3 12.2 %cholesky.217 = f32[128,128]{1,0:T(8,128)S(1)} custom-call(f32[128,128]{1,0:T(8,128)S(1)} %cholesky.270), custom_call_target="Cholesky" | custom-call | tf_op jit(solution)/shard_map/jit(cholesky)/cholesky | solution.py:39
  192.4 9.8 %custom-call.31 = f32[1,128,128]{1,2,0:T(8,128)S(1)} custom-call(f32[1,128,128]{2,1,0:T(8,128)S(1)} %get-tuple-element.30), custom_call_target="InvertDiagBlocksLowerTriangular" | custom-call | tf_op jit(solution)/shard_map/jit(cholesky)/cholesky | solution.py:39
  202.3 0.3 convolution_dynamic-update-slice_fusion
  202.5 0.4 convolution_subtract_fusion.4
  202.9 11.7 %cholesky.238 = f32[128,128]{1,0:T(8,128)S(1)} custom-call(f32[128,128]{1,0:T(8,128)S(1)} %cholesky.275), custom_call_target="Cholesky" | custom-call | tf_op jit(solution)/shard_map/jit(cholesky)/cholesky | solution.py:39
  214.7 0.7 compare_reduce_fusion.1
  215.3 9.8 %custom-call.32 = f32[1,128,128]{1,2,0:T(8,128)S(1)} custom-call(f32[1,128,128]{2,1,0:T(8,128)S(1)} %get-tuple-element.27), custom_call_target="InvertDiagBlocksLowerTriangular" | custom-call | tf_op jit(solution)/shard_map/jit(cholesky)/cholesky | solution.py:39
  225.1 0.2 convolution_dynamic-update-slice_fusion.1
  225.4 0.4 convolution_subtract_fusion.5
  225.7 11.9 %cholesky.255 = f32[128,128]{1,0:T(8,128)S(1)} custom-call(f32[128,128]{1,0:T(8,128)S(1)} %convolution_subtract_fusion.5), custom_call_target="Cholesky" | custom-call | tf_op jit(solution)/shard_map/jit(cholesky)/cholesky | solution.py:39
  237.6 0.7 compare_reduce_fusion
  238.3 0.7 compare_reduce_fusion.2
  241.6 0.1 select_select_fusion
  241.7 10.3 %while.1 = (s32[]{:T(128)}, f32[512,512]{1,0:T(8,128)S(1)}, s32[4,2]{0,1:T(2,128)S(1)}, f32[4,128,128]{2,1,0:T(8,128)}, s32[]{:T(128)}) while((s32[]{:T(128)}, f32[512,512]{1,0:T(8,128)S(1)}, s32[4,2]{0,1:T(2,128)S(1)}, f32[4,128,128]{2,1,0:T(8,128)}, s32[]{:T(128)}) %tuple.33), condition=%wide.while_cond, body=%wide.while_body.sunk | while | flops 2 | bytes 132205 | solution.py:40
  241.7 0.1 constant_dynamic-slice_fusion.2
  241.8 0.5 fusion.60
  242.3 2.0 bitcast_dynamic-update-slice_fusion.2
  244.3 0.1 constant_dynamic-slice_fusion.2
  244.4 0.5 fusion.60
  244.9 2.0 bitcast_dynamic-update-slice_fusion.2
  246.9 0.1 constant_dynamic-slice_fusion.2
  247.0 0.5 fusion.60
  247.5 2.0 bitcast_dynamic-update-slice_fusion.2
  249.5 0.1 constant_dynamic-slice_fusion.2
  249.5 0.5 fusion.60
  250.1 2.0 bitcast_dynamic-update-slice_fusion.2
  252.0 40.2 %custom-call.33 = f32[4,128,128]{1,2,0:T(8,128)S(1)} custom-call(f32[4,128,128]{2,1,0:T(8,128)} %get-tuple-element.9), custom_call_target="InvertDiagBlocksLowerTriangular" | custom-call | tf_op jit(solution)/shard_map/triangular_solve | solution.py:40
  292.2 2.4 fusion.15
  294.7 3.0 convolution_subtract_fusion.2
  297.7 1.1 fusion.37
  298.8 3.5 convolution_subtract_fusion.1
  302.4 1.1 fusion.35
  303.5 6.6 %fusion.6 = f32[128,2048]{0,1:T(8,128)S(1)} fusion(f32[128,2048]{1,0:T(8,128)S(1)} %fusion.35, f32[128,2048]{1,0:T(8,128)S(1)} %fusion.37, f32[128,2048]{1,0:T(8,128)S(1)} %fusion.15, f32[512,2048]{0,1:T(8,128)S(1)} %bitcast.61, f32[512,512]{1,0:T(8,128)} %copy-done.6), kind=kOutput, calls=%fused_computation.12 | convolution fusion | flops 1209794560 | bytes 5439488 | tf_op jit(solution)/shard_map/triangular_solve | solution.py:40
  310.1 1.1 fusion.34
  311.2 1.0 copy-done.5
  312.2 11.6 %fusion.9 = f32[512,768]{1,0:T(8,128)} fusion(f32[2048,768]{1,0:T(8,128)S(1)} %bitcast.63, f32[128,2048]{1,0:T(8,128)S(1)} %fusion.34, f32[128,2048]{1,0:T(8,128)S(1)} %fusion.35, f32[128,2048]{1,0:T(8,128)S(1)} %fusion.37, f32[128,2048]{1,0:T(8,128)S(1)} %fusion.15), kind=kOutput, calls=%fused_computation.15 | convolution fusion | flops 9666822144 | bytes 12058624 | tf_op jit(solution)/shard_map/dot_general | solution.py:59
  323.8 77.3 %all-reduce.6.cloned.1.call-done = f32[512,768]{1,0:T(8,128)} async-done(((f32[512,768]{1,0:T(8,128)}), f32[512,768]{1,0:T(8,128)}) %all-reduce.6.cloned.1.call-update) | async-done | bytes 1572880 | tf_op jit(solution)/shard_map/psum | solution.py:62
  401.0 23.9 %convolution_subtract_fusion = f32[2048,768]{1,0:T(8,128)} fusion(f32[2048,768]{1,0:T(8,128)} %multiply_multiply_fusion, f32[512,768]{1,0:T(8,128)} %all-reduce.6.cloned.1.call-done, f32[128,2048]{1,0:T(8,128)} %copy-done.5, f32[128,2048]{1,0:T(8,128)S(1)} %fusion.35, f32[128,2048]{1,0:T(8,128)S(1)} %fusion.37, f32[128,2048]{1,0:T(8,128)S(1)} %fusion.15), kind=kOutput, calls=%fused_computation.5 | convolution fusion | flops 9668395008 | bytes 18350080 | tf_op jit(solution)/shard_map/dot_general | solution.py:44
  424.9 1.1 copy.39
  (30 shorter events, 0.3 us)
Async XLA Ops:
  7.2 57.1 %all-gather.4.cloned.1.call-start = ((), (), s32[]{:S(2)}) async-start(), calls=%async_computation | async-start | bytes 3784704 | tf_op jit(solution)/shard_map/all_gather | solution.py:15
  9.5 145.4 %all-reduce.4.cloned.1.call-start = ((), (), s32[]{:S(2)}) async-start(), calls=%async_computation.1 | async-start | bytes 2097152 | tf_op jit(solution)/shard_map/psum | solution.py:57
  64.3 3.4 copy-start.2
  69.0 1.9 copy-start
  79.0 322.0 %all-reduce.6.cloned.1.call-start = ((), (), s32[]{:S(2)}) async-start(), calls=%async_computation.2 | async-start | bytes 3145728 | tf_op jit(solution)/shard_map/psum | solution.py:62
  79.3 2.4 copy-start.3
  252.0 46.8 %copy-start.6 = (f32[512,512]{1,0:T(8,128)}, f32[512,512]{1,0:T(8,128)S(1)}, u32[]{:S(2)}) copy-start(f32[512,512]{1,0:T(8,128)S(1)} %get-tuple-element.92) | copy-start | bytes 3145732
  292.2 6.6 %copy-start.1 = (f32[2048,512]{1,0:T(8,128)S(1)}, f32[2048,512]{1,0:T(8,128)}, u32[]{:S(2)}) copy-start(f32[2048,512]{1,0:T(8,128)} %copy-done) | copy-start | bytes 12582916
  298.8 13.4 %slice-start = ((s8[6291456]{0:T(1024)(128)(4,1)}), s8[4194304]{0:T(1024)(128)(4,1)S(1)}, s32[]{:S(2)}) async-start(s8[6291456]{0:T(1024)(128)(4,1)} %bitcast.62), calls=%async_computation.3 | async-start | bytes 8388608
  303.4 8.7 %slice-start.1 = ((s8[6291456]{0:T(1024)(128)(4,1)}), s8[2097152]{0:T(1024)(128)(4,1)S(1)}, s32[]{:S(2)}) async-start(s8[6291456]{0:T(1024)(128)(4,1)} %bitcast.62), calls=%async_computation.4 | async-start | bytes 4194304
  311.2 1.0 copy-start.5
  401.0 23.9 %copy-start.4 = (f32[512,768]{1,0:T(8,128)S(1)}, f32[512,768]{1,0:T(8,128)}, u32[]{:S(2)}) copy-start(f32[512,768]{1,0:T(8,128)} %all-reduce.6.cloned.1.call-done) | copy-start | bytes 4718596
Sparse Core Ops, SparseCore 0:
  11.1 53.1 all-gather.3
  79.1 75.7 all-reduce.3
  323.9 77.1 all-reduce.5
where the time goes:
time: 441 us; the launch traced here: 433 us
  waiting for transfers between devices  174 us (39%)
  other arithmetic  124 us (28%)
  matrix products  74.6 us (17%)
  blocking collectives  24.6 us (6%)
  local copies, waits for them, and re-layouts  18.3 us (4%)
  between operations  17.1 us (4%)
    another operation x14, other arithmetic, orthonormal(): lower_factor = jnp.linalg.cholesky(gram_sum)  79 us
    psum x1, waiting for transfers between devices, shards(): coefficients = lax.psum(local_rows, 'row')  77.3 us
    psum x1, waiting for transfers between devices, shards(): gram_sum = lax.psum(local_gram, 'row')  68.5 us
    another operation x3, other arithmetic, orthonormal(): lax.linalg.triangular_solve(lower_factor, panel_cols.T, left_side=True, l...  40.3 us
    all_gather x1, waiting for transfers between devices, in_one_piece(): result = lax.all_gather(both, axis, axis=dim, tiled=True)  28.7 us
    all_gather x1, blocking collectives, picked(): lax.all_gather(array, axis)  24.6 us
    dot_general x1, matrix products, remove_span(): jnp.dot(basis_t.T, top_rows, precision=lax.Precision.HIGHEST, preferred_e...  23.9 us
    another operation x7, matrix products, orthonormal(): lax.linalg.triangular_solve(lower_factor, panel_cols.T, left_side=True, l...  18.9 us
  transfers between devices with their start and end apart: 3, of which 3 were waited for; matrix products, arithmetic and copies ran while one was open for 2% of the time, Pallas kernels for 0%

commit v1 on v0

--- a/solution.py
+++ b/solution.py
@@ -59,7 +59,7 @@
     local_rows = jnp.dot(
         basis_t, design, precision=lax.Precision.HIGHEST, preferred_element_type=jnp.float32
     )
-    coefficients = lax.psum(local_rows, "row")
+    coefficients = jnp.sum(lax.all_gather(local_rows, "row"), axis=0)
     residual = remove_span(design, basis_t, coefficients)
     return (coefficients, residual)
 

time: 441 us -> 502 us (1.14)
  waiting for transfers between devices: 174 us -> 229 us
  other arithmetic: 124 us -> 131 us
    all_gather x0 -> x1, waiting for transfers between devices: none -> 132 us  [shards(): coefficients = jnp.sum(lax.all_gather(local_rows, 'row'), axis=0)]
    psum x1 -> x0, waiting for transfers between devices: 77.3 us -> none  [shards(): coefficients = lax.psum(local_rows, 'row')]
    reduce_sum x0 -> x1, other arithmetic: none -> 6.92 us  [shards(): coefficients = jnp.sum(lax.all_gather(local_rows, 'row'), axis=0)]
where the time goes in v1:
time: 502 us; the launch traced here: 493 us
  waiting for transfers between devices  229 us (46%)
  other arithmetic  131 us (26%)
  matrix products  74.2 us (15%)
  blocking collectives  24.6 us (5%)
  local copies, waits for them, and re-layouts  17.2 us (3%)
  between operations  16.9 us (3%)
    all_gather x1, waiting for transfers between devices, shards(): coefficients = jnp.sum(lax.all_gather(local_rows, 'row'), axis=0)  132 us
    another operation x14, other arithmetic, orthonormal(): lower_factor = jnp.linalg.cholesky(gram_sum)  79 us
    psum x1, waiting for transfers between devices, shards(): gram_sum = lax.psum(local_gram, 'row')  68.3 us
    another operation x3, other arithmetic, orthonormal(): lax.linalg.triangular_solve(lower_factor, panel_cols.T, left_side=True, l...  40.3 us
    all_gather x1, waiting for transfers between devices, in_one_piece(): result = lax.all_gather(both, axis, axis=dim, tiled=True)  28.7 us
    all_gather x1, blocking collectives, picked(): lax.all_gather(array, axis)  24.6 us
    dot_general x1, matrix products, remove_span(): jnp.dot(basis_t.T, top_rows, precision=lax.Precision.HIGHEST, preferred_e...  23.5 us
    another operation x7, matrix products, orthonormal(): lax.linalg.triangular_solve(lower_factor, panel_cols.T, left_side=True, l...  18.8 us
  transfers between devices with their start and end apart: 3, of which 3 were waited for; matrix products, arithmetic and copies ran while one was open for 2% of the time, Pallas kernels for 0%

profile of v1, /device:TPU:2, one launch (start us, length us, event | category | flops | bytes accessed | tf_op | source)
XLA Modules:
  0.0 493.1 jit_solution(16940532252885069303)
XLA Ops:
  7.2 0.0 all-gather.6.cloned.1.call-start
  7.2 0.8 copy.12
  8.0 1.5 pad_maximum_fusion.3
  9.5 0.0 all-gather.6.cloned.1.call-update
  9.5 0.0 all-reduce.3.cloned.1.call-start
  9.5 0.7 slice_bitcast_fusion.8
  10.2 24.6 %all-gather.2 = s32[32,2,512]{2,1,0:T(2,128)S(1)} all-gather(s32[1,2,512]{2,1,0:T(2,128)S(1)} %slice_bitcast_fusion.8), channel_id=2, replica_groups=mesh['row'=8,'col'=32] {'col'}, dimensions={0}, use_global_device_ids=true | all-gather | bytes 135168 | tf_op jit(solution)/shard_map/all_gather | solution.py:23
  34.8 0.8 slice_reduce_fusion
  35.6 28.7 %all-gather.6.cloned.1.call-done = bf16[2048,769]{1,0:T(8,128)(2,1)} async-done(((bf16[64,769]{1,0:T(8,128)(2,1)}), bf16[2048,769]{1,0:T(8,128)(2,1)}) %all-gather.6.cloned.1.call-update) | async-done | bytes 3149840 | tf_op jit(solution)/shard_map/all_gather | solution.py:15
  64.3 1.4 convert_reduce_fusion
  65.7 2.0 fusion.20
  67.7 1.3 multiply_multiply_fusion.1
  69.0 1.9 copy-done
  70.9 8.0 %fusion.49 = f32[512,512]{0,1:T(8,128)} fusion(f32[2048,512]{1,0:T(8,128)S(1)} %multiply_multiply_fusion.1), kind=kOutput, calls=%fused_computation.94 | convolution fusion | flops 6442450944 | bytes 5242880 | tf_op jit(solution)/shard_map/dot_general | solution.py:54
  79.0 0.5 all-gather.8.cloned.1.call-start
  79.5 2.4 fusion.18
  81.9 4.7 multiply_multiply_fusion
  86.6 68.3 %all-reduce.3.cloned.1.call-done = f32[512,512]{0,1:T(8,128)} async-done(((f32[512,512]{0,1:T(8,128)}), f32[512,512]{0,1:T(8,128)}) %all-reduce.3.cloned.1.call-update) | async-done | bytes 1048592 | tf_op jit(solution)/shard_map/psum | solution.py:57
  154.9 1.6 copy.14
  156.5 1.4 fusion.17
  158.0 11.7 %cholesky.104 = f32[128,128]{1,0:T(8,128)S(1)} custom-call(f32[128,128]{1,0:T(8,128)S(1)} %cholesky.266), custom_call_target="Cholesky" | custom-call | tf_op jit(solution)/shard_map/jit(cholesky)/cholesky | solution.py:39
  169.7 9.8 %custom-call.30 = f32[1,128,128]{1,2,0:T(8,128)S(1)} custom-call(f32[1,128,128]{2,1,0:T(8,128)S(1)} %get-tuple-element.33), custom_call_target="InvertDiagBlocksLowerTriangular" | custom-call | tf_op jit(solution)/shard_map/jit(cholesky)/cholesky | solution.py:39
  179.5 0.1 cholesky.224
  179.6 0.3 constant_dynamic-update-slice_fusion.3
  180.0 0.3 convolution_subtract_fusion.3
  180.3 11.9 %cholesky.217 = f32[128,128]{1,0:T(8,128)S(1)} custom-call(f32[128,128]{1,0:T(8,128)S(1)} %cholesky.270), custom_call_target="Cholesky" | custom-call | tf_op jit(solution)/shard_map/jit(cholesky)/cholesky | solution.py:39
  192.2 9.8 %custom-call.31 = f32[1,128,128]{1,2,0:T(8,128)S(1)} custom-call(f32[1,128,128]{2,1,0:T(8,128)S(1)} %get-tuple-element.30), custom_call_target="InvertDiagBlocksLowerTriangular" | custom-call | tf_op jit(solution)/shard_map/jit(cholesky)/cholesky | solution.py:39
  202.0 0.3 convolution_dynamic-update-slice_fusion
  202.3 0.4 convolution_subtract_fusion.4
  202.7 11.7 %cholesky.238 = f32[128,128]{1,0:T(8,128)S(1)} custom-call(f32[128,128]{1,0:T(8,128)S(1)} %cholesky.275), custom_call_target="Cholesky" | custom-call | tf_op jit(solution)/shard_map/jit(cholesky)/cholesky | solution.py:39
  214.5 0.7 compare_reduce_fusion.1
  215.1 9.8 %custom-call.32 = f32[1,128,128]{1,2,0:T(8,128)S(1)} custom-call(f32[1,128,128]{2,1,0:T(8,128)S(1)} %get-tuple-element.27), custom_call_target="InvertDiagBlocksLowerTriangular" | custom-call | tf_op jit(solution)/shard_map/jit(cholesky)/cholesky | solution.py:39
  224.9 0.2 convolution_dynamic-update-slice_fusion.1
  225.1 0.4 convolution_subtract_fusion.5
  225.5 12.1 %cholesky.255 = f32[128,128]{1,0:T(8,128)S(1)} custom-call(f32[128,128]{1,0:T(8,128)S(1)} %convolution_subtract_fusion.5), custom_call_target="Cholesky" | custom-call | tf_op jit(solution)/shard_map/jit(cholesky)/cholesky | solution.py:39
  237.6 0.7 compare_reduce_fusion
  238.3 0.7 compare_reduce_fusion.2
  241.6 0.1 select_select_fusion
  241.7 10.3 %while.1 = (s32[]{:T(128)}, f32[512,512]{1,0:T(8,128)S(1)}, s32[4,2]{0,1:T(2,128)S(1)}, f32[4,128,128]{2,1,0:T(8,128)}, s32[]{:T(128)}) while((s32[]{:T(128)}, f32[512,512]{1,0:T(8,128)S(1)}, s32[4,2]{0,1:T(2,128)S(1)}, f32[4,128,128]{2,1,0:T(8,128)}, s32[]{:T(128)}) %tuple.33), condition=%wide.while_cond, body=%wide.while_body.sunk | while | flops 2 | bytes 132205 | solution.py:40
  241.8 0.1 constant_dynamic-slice_fusion.2
  241.8 0.5 fusion.60
  242.4 2.0 bitcast_dynamic-update-slice_fusion.2
  244.3 0.1 constant_dynamic-slice_fusion.2
  244.4 0.5 fusion.60
  244.9 2.0 bitcast_dynamic-update-slice_fusion.2
  246.9 0.1 constant_dynamic-slice_fusion.2
  247.0 0.5 fusion.60
  247.5 2.0 bitcast_dynamic-update-slice_fusion.2
  249.5 0.1 constant_dynamic-slice_fusion.2
  249.6 0.5 fusion.60
  250.1 2.0 bitcast_dynamic-update-slice_fusion.2
  252.1 40.2 %custom-call.33 = f32[4,128,128]{1,2,0:T(8,128)S(1)} custom-call(f32[4,128,128]{2,1,0:T(8,128)} %get-tuple-element.9), custom_call_target="InvertDiagBlocksLowerTriangular" | custom-call | tf_op jit(solution)/shard_map/triangular_solve | solution.py:40
  292.2 2.4 fusion.15
  294.7 3.0 convolution_subtract_fusion.2
  297.7 1.1 fusion.37
  298.8 3.5 convolution_subtract_fusion.1
  302.4 1.1 fusion.35
  303.5 6.6 %fusion.6 = f32[128,2048]{0,1:T(8,128)S(1)} fusion(f32[128,2048]{1,0:T(8,128)S(1)} %fusion.35, f32[128,2048]{1,0:T(8,128)S(1)} %fusion.37, f32[128,2048]{1,0:T(8,128)S(1)} %fusion.15, f32[512,2048]{0,1:T(8,128)S(1)} %bitcast.62, f32[512,512]{1,0:T(8,128)} %copy-done.5), kind=kOutput, calls=%fused_computation.12 | convolution fusion | flops 1209794560 | bytes 5439488 | tf_op jit(solution)/shard_map/triangular_solve | solution.py:40
  310.1 1.1 fusion.34
  311.2 1.0 copy-done.4
  312.2 11.6 %fusion.9 = f32[512,768]{1,0:T(8,128)} fusion(f32[2048,768]{1,0:T(8,128)S(1)} %bitcast.64, f32[128,2048]{1,0:T(8,128)S(1)} %fusion.34, f32[128,2048]{1,0:T(8,128)S(1)} %fusion.35, f32[128,2048]{1,0:T(8,128)S(1)} %fusion.37, f32[128,2048]{1,0:T(8,128)S(1)} %fusion.15), kind=kOutput, calls=%fused_computation.15 | convolution fusion | flops 9666822144 | bytes 12058624 | tf_op jit(solution)/shard_map/dot_general | solution.py:59
  323.8 132.1 %all-gather.8.cloned.1.call-done = f32[4096,768]{1,0:T(8,128)} async-done(((f32[512,768]{1,0:T(8,128)}), f32[4096,768]{1,0:T(8,128)}) %all-gather.8.cloned.1.call-update) | async-done | bytes 12582928 | tf_op jit(solution)/shard_map/all_gather | solution.py:62
  455.9 6.9 %reduce_sum.9 = f32[512,768]{1,0:T(8,128)} reduce(f32[8,512,768]{2,1,0:T(8,128)} %bitcast.65, f32[]{:T(128)} %constant.143.clone.1), dimensions={0}, to_apply=%region_9.10 | reduce | flops 2752512 | bytes 14155780 | tf_op jit(solution)/shard_map/reduce_sum | solution.py:62
  462.8 23.5 %convolution_subtract_fusion = f32[2048,768]{1,0:T(8,128)} fusion(f32[2048,768]{1,0:T(8,128)} %multiply_multiply_fusion, f32[512,768]{1,0:T(8,128)} %reduce_sum.9, f32[128,2048]{1,0:T(8,128)} %copy-done.4, f32[128,2048]{1,0:T(8,128)S(1)} %fusion.35, f32[128,2048]{1,0:T(8,128)S(1)} %fusion.37, f32[128,2048]{1,0:T(8,128)S(1)} %fusion.15), kind=kOutput, calls=%fused_computation.5 | convolution fusion | flops 9668395008 | bytes 18350080 | tf_op jit(solution)/shard_map/dot_general | solution.py:44
  (28 shorter events, 0.2 us)
Async XLA Ops:
  7.2 57.1 %all-gather.6.cloned.1.call-start = ((), (), s32[]{:S(2)}) async-start(), calls=%async_computation | async-start | bytes 3784704 | tf_op jit(solution)/shard_map/all_gather | solution.py:15
  9.5 145.4 %all-reduce.3.cloned.1.call-start = ((), (), s32[]{:S(2)}) async-start(), calls=%async_computation.1 | async-start | bytes 2097152 | tf_op jit(solution)/shard_map/psum | solution.py:57
  64.3 3.4 copy-start.2
  69.0 1.9 copy-start
  79.0 376.9 %all-gather.8.cloned.1.call-start = ((), (), s32[]{:S(2)}) async-start(), calls=%async_computation.2 | async-start | bytes 14155776 | tf_op jit(solution)/shard_map/all_gather | solution.py:62
  79.5 2.4 copy-start.3
  252.1 46.8 %copy-start.5 = (f32[512,512]{1,0:T(8,128)}, f32[512,512]{1,0:T(8,128)S(1)}, u32[]{:S(2)}) copy-start(f32[512,512]{1,0:T(8,128)S(1)} %get-tuple-element.90) | copy-start | bytes 3145732
  292.2 6.6 %copy-start.1 = (f32[2048,512]{1,0:T(8,128)S(1)}, f32[2048,512]{1,0:T(8,128)}, u32[]{:S(2)}) copy-start(f32[2048,512]{1,0:T(8,128)} %copy-done) | copy-start | bytes 12582916
  298.8 13.4 %slice-start = ((s8[6291456]{0:T(1024)(128)(4,1)}), s8[4194304]{0:T(1024)(128)(4,1)S(1)}, s32[]{:S(2)}) async-start(s8[6291456]{0:T(1024)(128)(4,1)} %bitcast.63), calls=%async_computation.3 | async-start | bytes 8388608
  303.5 8.8 %slice-start.1 = ((s8[6291456]{0:T(1024)(128)(4,1)}), s8[2097152]{0:T(1024)(128)(4,1)S(1)}, s32[]{:S(2)}) async-start(s8[6291456]{0:T(1024)(128)(4,1)} %bitcast.63), calls=%async_computation.4 | async-start | bytes 4194304
  311.2 1.1 copy-start.4
Sparse Core Ops, SparseCore 0:
  11.1 53.1 all-gather.5
  79.1 75.7 all-reduce.2
  323.9 131.9 all-gather.7
